TPU v7x, 768 devices: a whole 4x8x12 slice. The times are simulated.
768 devices in a mesh: freq: 16 (over y_lo, x), rtile: 24 (over z, core), rep: 2 (over y_hi).
Axes of the slice: x: 4, y: 8 (y_hi: 2, y_lo: 4; y = y_hi * 4 + y_lo), z: 12, core: 2. Of those that a mesh axis runs over, the one named last changes fastest.
Arguments:
- model: bfloat16 [24, 512, 32, 1024], P('rtile', 'freq'), may hold values from -0.1796875 to 0.1796875
- green_left: bfloat16 [2, 48, 8, 48, 48, 256], P(None, 'freq', 'rep', 'rtile'), may hold values from -0.09375 to 0.09375
- green_right: bfloat16 [2, 48, 8, 48, 48, 256], P(None, 'freq', 'rep', 'rtile'), may hold values from -0.25 to 0.25
- ranks: int32 [48, 8, 48], P('freq', 'rep', 'rtile'), may hold values from 8 to 48
- data: float32 [2, 1536, 2048], P(None, ('freq', 'rtile'), 'rep'), may hold values from -3 to 3
Outputs:
- residual: float32 [2, 1536, 2048], P(None, ('freq', 'rtile'), 'rep')
- gradient: bfloat16 [24, 512, 32, 1024], P('rtile', ('freq', 'rep'))
All inputs are finite; a program needn't handle non-finite values.
Results may differ from a plain program's by a relative error of at most 0.014.
Values may be sent and summed in bfloat16 or wider, within the bound.
A program may use at most 32 MiB of HBM per device.

v0:
```python
import math

import jax
import jax.numpy as jnp
from jax import lax
from jax.sharding import PartitionSpec as P


def tables(count, length):
    freq_bins = 1 + jnp.arange(count, dtype=jnp.int32)
    samples = jnp.arange(length, dtype=jnp.int32)
    phases = (samples[:, None] * freq_bins[None, :] % length).astype(jnp.float32) * (
        2.0 * math.pi / length
    )
    return (jnp.cos(phases).astype(jnp.bfloat16), (-jnp.sin(phases)).astype(jnp.bfloat16))


def product(form, first, second):
    return jnp.einsum(form, first, second, preferred_element_type=jnp.float32)


def shards(model, green_left, green_right, ranks, data):
    freq_count = lax.axis_size("freq")
    freq_local = ranks.shape[0]
    freq_total = freq_local * freq_count
    length = model.shape[-1]
    rhs_count = model.shape[2]
    rank_size = green_left.shape[4]
    tile_size = green_left.shape[5]
    row_tiles = green_left.shape[2]
    col_tiles = green_left.shape[3]
    cosine, sine_neg = tables(freq_total, length)
    own_traces = model[0]
    spectrum = jnp.stack(
        [product("mrt,tq->qmr", own_traces, cosine), product("mrt,tq->qmr", own_traces, sine_neg)]
    ).astype(jnp.bfloat16)
    spectrum = lax.all_to_all(spectrum, "freq", split_axis=1, concat_axis=2, tiled=True)
    spectrum = spectrum.reshape(2, freq_local, col_tiles, tile_size, rhs_count)
    rank_mask = (jnp.arange(rank_size, dtype=jnp.int32) < ranks[..., None]).astype(jnp.float32)[
        ..., None
    ]
    proj_re = product("fijkn,fjnr->fijkr", green_right[0], spectrum[0]) + product(
        "fijkn,fjnr->fijkr", green_right[1], spectrum[1]
    )
    proj_im = product("fijkn,fjnr->fijkr", green_right[0], spectrum[1]) - product(
        "fijkn,fjnr->fijkr", green_right[1], spectrum[0]
    )
    proj_re = (proj_re * rank_mask).astype(jnp.bfloat16)
    proj_im = (proj_im * rank_mask).astype(jnp.bfloat16)
    out_re = product("fijks,fijkr->fris", green_left[0], proj_re) - product(
        "fijks,fijkr->fris", green_left[1], proj_im
    )
    out_im = product("fijks,fijkr->fris", green_left[0], proj_im) + product(
        "fijks,fijkr->fris", green_left[1], proj_re
    )
    pair_count = freq_local * rhs_count
    predicted = jnp.stack([out_re, out_im]).reshape(2, pair_count, row_tiles * tile_size)
    own_sums = lax.psum_scatter(predicted, "rtile", scatter_dimension=1, tiled=True)
    residual = own_sums - data
    misfit_low = lax.all_gather(residual.astype(jnp.bfloat16), "rtile", axis=1, tiled=True)
    misfit_low = misfit_low.reshape(2, freq_local, rhs_count, row_tiles, tile_size)
    back_re = product("fijks,fris->fijkr", green_left[0], misfit_low[0]) + product(
        "fijks,fris->fijkr", green_left[1], misfit_low[1]
    )
    back_im = product("fijks,fris->fijkr", green_left[0], misfit_low[1]) - product(
        "fijks,fris->fijkr", green_left[1], misfit_low[0]
    )
    back_re = (back_re * rank_mask).astype(jnp.bfloat16)
    back_im = (back_im * rank_mask).astype(jnp.bfloat16)
    grad_re = product("fijkn,fijkr->fjnr", green_right[0], back_re) - product(
        "fijkn,fijkr->fjnr", green_right[1], back_im
    )
    grad_im = product("fijkn,fijkr->fjnr", green_right[0], back_im) + product(
        "fijkn,fijkr->fjnr", green_right[1], back_re
    )
    partial_grad = jnp.stack([grad_re, grad_im]).reshape(
        2, freq_local, col_tiles * tile_size, rhs_count
    )
    arrived = lax.all_to_all(partial_grad, ("freq", "rep"), split_axis=2, concat_axis=1, tiled=True)
    group_size = arrived.shape[2]
    arrived = arrived.reshape(2, freq_count, 2, freq_local, group_size, rhs_count)
    grad_spec = (
        jnp.sum(arrived, axis=2).reshape(2, freq_total, group_size, rhs_count).astype(jnp.bfloat16)
    )
    gradient = product("qmr,tq->mrt", grad_spec[0], cosine) + product(
        "qmr,tq->mrt", grad_spec[1], sine_neg
    )
    return (residual, gradient.astype(jnp.bfloat16)[None])


def solution(mesh):
    return jax.shard_map(
        shards,
        mesh=mesh,
        in_specs=(
            P("rtile", "freq", None, None),
            P(None, "freq", "rep", "rtile", None, None),
            P(None, "freq", "rep", "rtile", None, None),
            P("freq", "rep", "rtile"),
            P(None, ("freq", "rtile"), "rep"),
        ),
        out_specs=(P(None, ("freq", "rtile"), "rep"), P("rtile", ("freq", "rep"), None, None)),
        check_vma=False,
    )
```

profile of v0, /device:TPU:1, one launch (start us, length us, event | category | flops | bytes accessed | tf_op | source)
XLA Modules:
  0.0 301.5 jit_solution(15682253097646769568)
XLA Ops:
  7.2 1.6 copy-done
  8.8 1.4 fusion.25
  10.2 1.4 fusion.28
  13.0 1.4 reshape.68
  14.4 8.0 %all-to-all-start = ((bf16[16,2,3072]{2,1,0:T(2,128)(2,1)}), bf16[16,2,3072]{2,1,0:T(2,128)(2,1)}, u32[]{:S(2)}, u32[]{:S(2)}) async-start(bf16[16,2,3072]{2,1,0:T(2,128)(2,1)} %reshape.68), calls=%async_computation | async-start | bytes 393216 | tf_op jit(solution)/shard_map/all_to_all | solution.py:37
  22.6 2.2 fusion.106
  24.8 6.1 %all-to-all-done = bf16[16,2,3072]{2,1,0:T(2,128)(2,1)} async-done(((bf16[16,2,3072]{2,1,0:T(2,128)(2,1)}), bf16[16,2,3072]{2,1,0:T(2,128)(2,1)}, u32[]{:S(2)}, u32[]{:S(2)}) %all-to-all-start) | async-done | bytes 196640 | tf_op jit(solution)/shard_map/all_to_all | solution.py:37
  33.4 1.9 squeeze.25
  37.9 1.4 fusion.23
  42.4 2.0 stack.34
  46.6 2.0 stack.33
  48.5 2.1 pad_maximum_fusion
  52.6 167.5 %all-reduce.3.cloned.1.call-done = f32[2,96,1024]{2,1,0:T(8,128)} async-done(((f32[2,96,1024]{2,1,0:T(8,128)}), f32[2,96,1024]{2,1,0:T(8,128)}) %all-reduce.3.cloned.1.call-update) | async-done | bytes 786448
  220.1 1.5 fusion.105
  221.6 25.1 %all_gather.3 = bf16[2,96,1024]{2,0,1:T(2,128)(2,1)S(1)} all-gather(bf16[2,4,1024]{2,0,1:T(2,128)(2,1)S(1)} %copy.125), channel_id=1, replica_groups=mesh['freq'=16,'rtile'=24,'rep'=2] {'rtile'}, dimensions={1}, use_global_device_ids=true | all-gather | bytes 409600 | tf_op jit(solution)/shard_map/all_gather | solution.py:60
  246.7 2.3 slice_reduce_fusion
  255.6 2.1 copy.137
  257.7 3.0 reshape.70
  260.7 21.7 %all_to_all.30 = f32[32,1,3072]{2,1,0:T(1,128)S(1)} all-to-all(f32[32,1,3072]{2,1,0:T(1,128)S(1)} %reshape.70), channel_id=1, replica_groups=mesh['freq'=16,'rtile'=24,'rep'=2] {'freq','rep'}, dimensions={0} | all-to-all | bytes 786432 | tf_op jit(solution)/shard_map/all_to_all | solution.py:79
  282.9 1.6 reduce.4
  284.4 2.5 reshape.71
  286.9 2.7 copy.138
  289.6 1.6 reduce_sum.9
  292.5 2.2 fusion.4
  (65 shorter events, 21.3 us)
Async XLA Ops:
  7.2 1.6 copy-start
  11.7 10.8 %copy-start.10 = (s32[3,4,2]{1,2,0:T(2,128)S(1)}, s32[3,4,2]{1,2,0:T(2,128)}, u32[]{:S(2)}) copy-start(s32[3,4,2]{1,2,0:T(2,128)} %param.8) | copy-start | bytes 292
  14.4 16.4 %all-to-all-start = ((bf16[16,2,3072]{2,1,0:T(2,128)(2,1)}), bf16[16,2,3072]{2,1,0:T(2,128)(2,1)}, u32[]{:S(2)}, u32[]{:S(2)}) async-start(bf16[16,2,3072]{2,1,0:T(2,128)(2,1)} %reshape.68), calls=%async_computation | async-start | bytes 393216 | tf_op jit(solution)/shard_map/all_to_all | solution.py:37
  22.5 197.6 %all-reduce.3.cloned.1.call-start = ((), (), s32[]{:S(2)}) async-start(), calls=%async_computation.2 | async-start | bytes 1572864
  24.8 12.6 %copy-start.2 = (bf16[1,3,4,2,48,256]{5,4,3,2,1,0:T(8,128)(2,1)}, bf16[1,3,4,2,48,256]{5,4,3,2,1,0:T(8,128)(2,1)S(1)}, u32[]{:S(2)}) copy-start(bf16[1,3,4,2,48,256]{5,4,3,2,1,0:T(8,128)(2,1)S(1)} %get-tuple-element.7) | copy-start | bytes 1769476
  36.0 1.9 copy-start.8
  36.0 1.9 copy-start.4
  37.4 1.9 copy-start.7
  37.8 1.9 copy-start.1
  48.5 171.6 %copy-start.9 = (f32[2,4,1024]{2,1,0:T(4,128)S(1)}, f32[2,4,1024]{2,1,0:T(4,128)}, u32[]{:S(2)}) copy-start(f32[2,4,1024]{2,1,0:T(4,128)} %param.9) | copy-start | bytes 98308
  250.9 0.9 copy-start.6
  252.2 1.1 copy-start.5
  253.3 1.1 copy-start.3
Sparse Core Ops, SparseCore 0:
  50.8 169.3 all-reduce.2
where the time goes:
time: 305 us; the launch traced here: 302 us
  waiting for transfers between devices  174 us (57%)
  blocking collectives  46.8 us (15%)
  local copies, waits for them, and re-layouts  35.5 us (12%)
  matrix products  15.5 us (5%)
  between operations  15.1 us (5%)
  starting transfers between devices  8.08 us (3%)
  other arithmetic  6.97 us (2%)
    unnamed x2, waiting for transfers between devices  168 us
    all_gather x1, blocking collectives, shards(): lax.all_gather(residual.astype(jnp.bfloat16), 'rtile', axis=1, tiled=True)  25.1 us
    all_to_all x1, blocking collectives, shards(): lax.all_to_all(partial_grad, ('freq', 'rep'), split_axis=2, concat_axis=1...  21.7 us
    dot_general x20, matrix products, product(): return jnp.einsum(form, first, second, preferred_element_type=jnp.float32)  15.5 us
    unnamed x27, local copies, waits for them, and re-layouts  12.3 us
    all_to_all x1, starting transfers between devices, shards(): lax.all_to_all(spectrum, 'freq', split_axis=1, concat_axis=2, tiled=True)  8.04 us
  transfers between devices with their start and end apart: 2, of which 2 were waited for; matrix products, arithmetic and copies ran while one was open for 1% of the time, Pallas kernels for 0%

commit v1 on v0

v1 whole, which is shorter than its diff:
```python
import functools

import jax
import jax.numpy as jnp
import ml_dtypes
import numpy as np
from jax import lax
from jax.experimental import pallas as pl
from jax.experimental.pallas import tpu as pltpu
from jax.sharding import PartitionSpec as P

MESH = pl.DeviceIdType.MESH
BF16 = jnp.bfloat16
F32 = jnp.float32
LAST = (((1,), (1,)), ((), ()))
PLAIN = (((1,), (0,)), ((), ()))


def tables(count, length):
    bins = 1 + np.arange(count, dtype=np.int64)
    phases = (bins[:, None] * np.arange(length, dtype=np.int64)[None, :] % length).astype(
        np.float32
    ) * np.float32(2.0 * np.pi / length)
    both = np.concatenate([np.cos(phases), -np.sin(phases)], axis=0)
    return both.astype(ml_dtypes.bfloat16)


def matmul(form, first, second):
    return lax.dot_general(first, second, form, preferred_element_type=F32)


def lanes(shape):
    return lax.broadcasted_iota(jnp.int32, shape, len(shape) - 1)


def rows(shape):
    return lax.broadcasted_iota(jnp.int32, shape, len(shape) - 2)


def chain_kernel(
    dims,
    model_ref,
    left_ref,
    right_ref,
    ranks_ref,
    data_ref,
    table_ref,
    residual_ref,
    spec_ref,
    traces,
    table,
    left,
    right,
    stage,
    send_a,
    recv_a,
    weights,
    send_r,
    recv_sib,
    send_z,
    recv_z,
    recv_d,
    back,
    grads,
    send_g,
    recv_g,
    load_sem,
    out_sem,
    a_sem,
    sib_sem,
    z_sem,
    d_sem,
    swap_sem,
    g_sem,
):
    n_freq, n_rtile, n_rep = dims
    n_z = n_rtile // 2
    n_slot = n_freq * n_rep
    me_f = lax.axis_index("freq")
    me_t = lax.axis_index("rtile")
    me_p = lax.axis_index("rep")
    me_slot = me_f * n_rep + me_p
    me_z = me_t // 2
    me_c = me_t % 2
    sibling = {"rtile": me_z * 2 + (1 - me_c)}
    group = model_ref.shape[1] // n_rep
    freq_local, row_tiles, col_tiles, rank_size, tile_size = right.shape[1:]

    def slot_device(slot):
        return {"freq": slot // n_rep, "rep": slot % n_rep}

    def z_device(z):
        return {"rtile": z * 2 + me_c}

    def slots_like(send_sem, recv_sem):
        most = recv_a.at[pl.ds(0, n_slot - 1)]
        return pltpu.make_async_remote_copy(
            src_ref=most,
            dst_ref=most,
            send_sem=send_sem,
            recv_sem=recv_sem,
            device_id=sibling,
            device_id_type=MESH,
        )

    def zs_like(send_sem, recv_sem):
        most = recv_z.at[pl.ds(0, n_z - 1)]
        return pltpu.make_async_remote_copy(
            src_ref=most,
            dst_ref=most,
            send_sem=send_sem,
            recv_sem=recv_sem,
            device_id=sibling,
            device_id_type=MESH,
        )

    model_load = pltpu.make_async_copy(
        model_ref.at[0, pl.ds(me_p * group, group)], traces, load_sem.at[0]
    )
    table_load = pltpu.make_async_copy(table_ref, table, load_sem.at[1])
    right_load = pltpu.make_async_copy(right_ref, right, load_sem.at[2])
    left_load = pltpu.make_async_copy(left_ref, left, load_sem.at[3])
    model_load.start()
    table_load.start()
    right_load.start()
    left_load.start()

    barrier = pltpu.get_barrier_semaphore()

    @pl.loop(1, n_slot)
    def _(step):
        pl.semaphore_signal(
            barrier, inc=1, device_id=slot_device((me_slot + step) % n_slot), device_id_type=MESH
        )

    @pl.loop(1, n_z)
    def _(step):
        pl.semaphore_signal(
            barrier, inc=1, device_id=z_device((me_z + step) % n_z), device_id_type=MESH
        )

    pl.semaphore_signal(barrier, inc=1, device_id=sibling, device_id_type=MESH)

    table_load.wait()
    model_load.wait()
    bins = n_freq * freq_local
    traces_2d = traces[...].reshape(group * traces.shape[1], traces.shape[2])
    spectra = matmul(LAST, table[...], traces_2d)
    quarter = lanes((bins, 128)) // 32
    for chunk in range(group // 4):
        re = spectra[:bins, chunk * 128 : (chunk + 1) * 128]
        im = spectra[bins:, chunk * 128 : (chunk + 1) * 128]
        first = jnp.where(
            quarter == 0,
            re,
            jnp.where(
                quarter == 1,
                pltpu.roll(im, 32, 1),
                jnp.where(quarter == 2, pltpu.roll(re, 32, 1), pltpu.roll(im, 64, 1)),
            ),
        )
        second = jnp.where(
            quarter == 0,
            pltpu.roll(re, 64, 1),
            jnp.where(
                quarter == 1,
                pltpu.roll(im, 96, 1),
                jnp.where(quarter == 2, pltpu.roll(re, 96, 1), im),
            ),
        )
        stage[pl.ds(2 * chunk, bins, stride=8), :] = first
        stage[pl.ds(2 * chunk + 1, bins, stride=8), :] = second
    band = freq_local * 8
    send_a[...] = stage[...].reshape(n_freq, band, 128).astype(BF16)

    pl.semaphore_wait(barrier, n_slot - 1 + n_z)

    def a_copy(target, source):
        return pltpu.make_async_remote_copy(
            src_ref=send_a.at[target // n_rep],
            dst_ref=recv_a.at[source],
            send_sem=out_sem.at[0],
            recv_sem=a_sem,
            device_id=slot_device(target),
            device_id_type=MESH,
        )

    @pl.loop(1, n_slot)
    def _(step):
        a_copy((me_slot + step) % n_slot, me_slot).start()

    recv_a[me_slot] = send_a[me_f]
    right_load.wait()
    left_load.wait()

    slots_like(out_sem.at[0], a_sem).wait_recv()

    per_tile = n_slot // col_tiles
    lane_p = lanes((row_tiles * rank_size, 128))
    row_k = rows((rank_size, 128))
    for f in range(freq_local):
        for j in range(col_tiles):
            arrived = recv_a[j * per_tile : (j + 1) * per_tile, f * 8 : (f + 1) * 8, :]
            arrived = arrived.astype(F32).reshape(per_tile * 8, 128)
            weights[pl.ds(0, per_tile * 8, stride=2), :] = arrived
            weights[pl.ds(1, per_tile * 8, stride=2), :] = pltpu.roll(arrived, 64, 1)
            columns = weights[...].astype(BF16)
            by_re = matmul(
                PLAIN, right[0, f, :, j].reshape(row_tiles * rank_size, tile_size), columns
            )
            by_im = matmul(
                PLAIN, right[1, f, :, j].reshape(row_tiles * rank_size, tile_size), columns
            )
            projected = by_re + jnp.where(
                lane_p < 32, pltpu.roll(by_im, 96, 1), -pltpu.roll(by_im, 32, 1)
            )
            for i in range(row_tiles):
                part = projected[i * rank_size : (i + 1) * rank_size]
                back[f, i, j * rank_size : (j + 1) * rank_size, :] = jnp.where(
                    row_k < ranks_ref[f, i, j], part, 0.0
                )
    low4 = rows((32, tile_size)) % 8 < 4
    for f in range(freq_local):
        for i in range(row_tiles):
            lhs = back[f, i].T[:64].astype(BF16)
            span = slice(i * tile_size, (i + 1) * tile_size)
            by_re = matmul(PLAIN, lhs, left[0, f, i].reshape(col_tiles * rank_size, tile_size))
            by_im = matmul(PLAIN, lhs, left[1, f, i].reshape(col_tiles * rank_size, tile_size))
            out_re = by_re[:32] - by_im[32:]
            out_im = by_re[32:] + by_im[:32]
            even = jnp.where(low4, out_re, pltpu.roll(out_im, 4, 0))
            odd = jnp.where(low4, pltpu.roll(out_re, 28, 0), out_im)
            send_r[0, f * 4 : (f + 1) * 4, :, span] = even.reshape(4, 8, tile_size).astype(BF16)
            send_r[1, f * 4 : (f + 1) * 4, :, span] = odd.reshape(4, 8, tile_size).astype(BF16)

    sib_copy = pltpu.make_async_remote_copy(
        src_ref=send_r.at[1 - me_c],
        dst_ref=recv_sib,
        send_sem=out_sem.at[1],
        recv_sem=sib_sem,
        device_id=sibling,
        device_id_type=MESH,
    )
    sib_copy.start()
    sib_copy.wait_recv()
    send_z[...] = (send_r[me_c].astype(F32) + recv_sib[...].astype(F32)).astype(BF16)

    def z_copy(target, source):
        return pltpu.make_async_remote_copy(
            src_ref=send_z.at[target],
            dst_ref=recv_z.at[source],
            send_sem=out_sem.at[2],
            recv_sem=z_sem,
            device_id=z_device(target),
            device_id_type=MESH,
        )

    @pl.loop(1, n_z)
    def _(step):
        z_copy((me_z + step) % n_z, me_z).start()

    recv_z[me_z] = send_z[me_z]

    zs_like(out_sem.at[2], z_sem).wait_recv()

    total = recv_z[0].astype(F32)
    for z in range(1, n_z):
        total = total + recv_z[z].astype(F32)
    residual_re = total[:4] - data_ref[0]
    residual_im = total[4:] - data_ref[1]
    residual_ref[0] = residual_re
    residual_ref[1] = residual_im
    recv_d[me_c, me_z] = jnp.concatenate([residual_re, residual_im], axis=0).astype(BF16)

    def d_copy(target, source):
        return pltpu.make_async_remote_copy(
            src_ref=recv_d.at[me_c, source],
            dst_ref=recv_d.at[me_c, source],
            send_sem=out_sem.at[3],
            recv_sem=d_sem,
            device_id=z_device(target),
            device_id_type=MESH,
        )

    @pl.loop(1, n_z)
    def _(step):
        d_copy((me_z + step) % n_z, me_z).start()

    zs_like(out_sem.at[3], d_sem).wait_recv()

    swap = pltpu.make_async_remote_copy(
        src_ref=recv_d.at[me_c],
        dst_ref=recv_d.at[me_c],
        send_sem=out_sem.at[4],
        recv_sem=swap_sem,
        device_id=sibling,
        device_id_type=MESH,
    )
    swap.start()
    swap.wait_recv()

    low4 = rows((32, recv_d.shape[3])) % 8 < 4
    row_k = rows((rank_size, 128))
    for f in range(freq_local):
        even = recv_d[0, f * 4 : (f + 1) * 4].astype(F32).reshape(32, -1)
        odd = recv_d[1, f * 4 : (f + 1) * 4].astype(F32).reshape(32, -1)
        mis_re = jnp.where(low4, even, pltpu.roll(odd, 4, 0))
        mis_im = jnp.where(low4, pltpu.roll(even, 28, 0), odd)
        top = jnp.concatenate([mis_re, mis_im, -mis_im, mis_re], axis=0).astype(BF16)
        low = jnp.concatenate([mis_im, -mis_re, mis_re, mis_im], axis=0).astype(BF16)
        for i in range(row_tiles):
            span = slice(i * tile_size, (i + 1) * tile_size)
            part = matmul(
                LAST, left[0, f, i].reshape(col_tiles * rank_size, tile_size), top[:, span]
            ) + matmul(
                LAST, left[1, f, i].reshape(col_tiles * rank_size, tile_size), low[:, span]
            )
            for j in range(col_tiles):
                grads[j, i * rank_size : (i + 1) * rank_size, :] = jnp.where(
                    row_k < ranks_ref[f, i, j], part[j * rank_size : (j + 1) * rank_size], 0.0
                )
        for j in range(col_tiles):
            lhs = grads[j].T.astype(BF16)
            spec_t = matmul(
                PLAIN, lhs[:64], right[0, f, :, j].reshape(row_tiles * rank_size, tile_size)
            ) + matmul(
                PLAIN, lhs[64:], right[1, f, :, j].reshape(row_tiles * rank_size, tile_size)
            )
            weights[:, :64] = spec_t.T
            even = weights[pl.ds(0, per_tile * 8, stride=2), :]
            odd = weights[pl.ds(1, per_tile * 8, stride=2), :]
            packed = jnp.where(lanes(even.shape) < 64, even, pltpu.roll(odd, 64, 1))
            send_g[j * per_tile : (j + 1) * per_tile, f * 8 : (f + 1) * 8, :] = packed.reshape(
                per_tile, 8, 128
            ).astype(BF16)

    def g_copy(target, source):
        return pltpu.make_async_remote_copy(
            src_ref=send_g.at[target],
            dst_ref=recv_g.at[source],
            send_sem=out_sem.at[5],
            recv_sem=g_sem,
            device_id=slot_device(target),
            device_id_type=MESH,
        )

    @pl.loop(1, n_slot)
    def _(step):
        g_copy((me_slot + step) % n_slot, me_slot).start()

    recv_g[me_slot] = send_g[me_slot]

    slots_like(out_sem.at[5], g_sem).wait_recv()

    for f in range(n_freq):
        both = recv_g[n_rep * f].astype(F32)
        for p in range(1, n_rep):
            both = both + recv_g[n_rep * f + p].astype(F32)
        stage[f * band : (f + 1) * band, :] = both
    for chunk in range(group // 4):
        first = stage[pl.ds(2 * chunk, bins, stride=8), :]
        second = stage[pl.ds(2 * chunk + 1, bins, stride=8), :]
        re = jnp.where(
            quarter == 0,
            first,
            jnp.where(
                quarter == 1,
                pltpu.roll(first, 96, 1),
                jnp.where(quarter == 2, pltpu.roll(second, 64, 1), pltpu.roll(second, 32, 1)),
            ),
        )
        im = jnp.where(
            quarter == 0,
            pltpu.roll(first, 96, 1),
            jnp.where(
                quarter == 1,
                pltpu.roll(first, 64, 1),
                jnp.where(quarter == 2, pltpu.roll(second, 32, 1), second),
            ),
        )
        spec_ref[:bins, chunk * 128 : (chunk + 1) * 128] = re.astype(BF16)
        spec_ref[bins:, chunk * 128 : (chunk + 1) * 128] = im.astype(BF16)

    slots_like(out_sem.at[0], a_sem).wait_send()
    zs_like(out_sem.at[2], z_sem).wait_send()
    zs_like(out_sem.at[3], d_sem).wait_send()
    slots_like(out_sem.at[5], g_sem).wait_send()
    sib_copy.wait_send()
    swap.wait_send()


def traces_kernel(spec_ref, table_ref, raw_ref, residual_ref, gradient_ref):
    residual_ref[...] = raw_ref[...]
    lhs = spec_ref[...].astype(F32).T.astype(BF16)
    out = matmul(PLAIN, lhs, table_ref[...])
    gradient_ref[...] = out.reshape(gradient_ref.shape).astype(BF16)


def shards(dims, model, green_left, green_right, ranks, data):
    n_freq, n_rtile, n_rep = dims
    n_z = n_rtile // 2
    n_slot = n_freq * n_rep
    _, receivers, rhs_count, length = model.shape
    group = receivers // n_rep
    freq_local = ranks.shape[0]
    row_tiles, col_tiles, rank_size, tile_size = green_left.shape[2:]
    bins = n_freq * freq_local
    sources = row_tiles * tile_size
    assert (rhs_count, tile_size, group, col_tiles) == (32, 256, 16, 2)
    assert n_z == freq_local * 4 and n_slot * group == col_tiles * tile_size
    table = jnp.asarray(tables(bins, length))
    band = freq_local * 8
    raw, spec = pl.pallas_call(
        functools.partial(chain_kernel, dims),
        out_shape=(
            jax.ShapeDtypeStruct(data.shape, F32),
            jax.ShapeDtypeStruct((2 * bins, group * rhs_count), BF16),
        ),
        in_specs=[
            pl.BlockSpec(memory_space=pl.ANY),
            pl.BlockSpec(memory_space=pl.ANY),
            pl.BlockSpec(memory_space=pl.ANY),
            pl.BlockSpec(memory_space=pltpu.SMEM),
            pl.BlockSpec(memory_space=pltpu.VMEM),
            pl.BlockSpec(memory_space=pl.ANY),
        ],
        out_specs=(
            pl.BlockSpec(memory_space=pltpu.VMEM),
            pl.BlockSpec(memory_space=pltpu.VMEM),
        ),
        scratch_shapes=[
            pltpu.VMEM((group, rhs_count, length), BF16),
            pltpu.VMEM((2 * bins, length), BF16),
            pltpu.VMEM(green_left.shape, BF16),
            pltpu.VMEM(green_right.shape, BF16),
            pltpu.VMEM((bins * 8, 128), F32),
            pltpu.VMEM((n_freq, band, 128), BF16),
            pltpu.VMEM((n_slot, band, 128), BF16),
            pltpu.VMEM((tile_size, 128), F32),
            pltpu.VMEM((2, n_z, 8, sources), BF16),
            pltpu.VMEM((n_z, 8, sources), BF16),
            pltpu.VMEM((n_z, 8, sources), BF16),
            pltpu.VMEM((n_z, 8, sources), BF16),
            pltpu.VMEM((2, n_z, 8, sources), BF16),
            pltpu.VMEM((freq_local, row_tiles, col_tiles * rank_size, 128), F32),
            pltpu.VMEM((col_tiles, row_tiles * rank_size, 128), F32),
            pltpu.VMEM((n_slot, band, 128), BF16),
            pltpu.VMEM((n_slot, band, 128), BF16),
            pltpu.SemaphoreType.DMA((4,)),
            pltpu.SemaphoreType.DMA((6,)),
            pltpu.SemaphoreType.DMA,
            pltpu.SemaphoreType.DMA,
            pltpu.SemaphoreType.DMA,
            pltpu.SemaphoreType.DMA,
            pltpu.SemaphoreType.DMA,
            pltpu.SemaphoreType.DMA,
        ],
        compiler_params=pltpu.CompilerParams(
            collective_id=0, has_side_effects=True, vmem_limit_bytes=48 * 1024 * 1024
        ),
    )(model, green_left, green_right, ranks, data, table)
    steps = 4
    residual, gradient = pl.pallas_call(
        traces_kernel,
        grid=(steps,),
        out_shape=(
            jax.ShapeDtypeStruct(data.shape, F32),
            jax.ShapeDtypeStruct((1, group, rhs_count, length), BF16),
        ),
        in_specs=[
            pl.BlockSpec((2 * bins, group * rhs_count // steps), lambda step: (0, step)),
            pl.BlockSpec((2 * bins, length), lambda step: (0, 0)),
            pl.BlockSpec(data.shape, lambda step: (0, 0, 0)),
        ],
        out_specs=(
            pl.BlockSpec(data.shape, lambda step: (0, 0, 0)),
            pl.BlockSpec((1, group // steps, rhs_count, length), lambda step: (0, step, 0, 0)),
        ),
    )(spec, table, raw)
    return (residual, gradient)


def solution(mesh):
    dims = tuple(mesh.shape[name] for name in ("freq", "rtile", "rep"))
    return jax.shard_map(
        functools.partial(shards, dims),
        mesh=mesh,
        in_specs=(
            P("rtile", "freq", None, None),
            P(None, "freq", "rep", "rtile", None, None),
            P(None, "freq", "rep", "rtile", None, None),
            P("freq", "rep", "rtile"),
            P(None, ("freq", "rtile"), "rep"),
        ),
        out_specs=(P(None, ("freq", "rtile"), "rep"), P("rtile", ("freq", "rep"), None, None)),
        check_vma=False,
    )
```

time: 305 us -> 73.6 us (0.24)
  waiting for transfers between devices: 174 us -> 0 us
  Pallas kernels: 0 us -> 64.6 us
  blocking collectives: 46.8 us -> 0 us
  local copies, waits for them, and re-layouts: 35.5 us -> 7.83 us
  matrix products: 15.5 us -> 0 us
  between operations: 15.1 us -> 0.65 us
  starting transfers between devices: 8.08 us -> 0 us
  other arithmetic: 6.97 us -> 0 us
    unnamed x2 -> x0, waiting for transfers between devices: 168 us -> none
    pallas_call x0 -> x2, Pallas kernels: none -> 64.6 us  [the longest x1 60.9 us: shards(): pl.pallas_call(functools.partial(chain_kernel, dims), out_shape=(jax.Shap...]
    all_gather x1 -> x0, blocking collectives: 25.1 us -> none  [shards(): lax.all_gather(residual.astype(jnp.bfloat16), 'rtile', axis=1, tiled=True)]
    all_to_all x1 -> x0, blocking collectives: 21.7 us -> none  [shards(): lax.all_to_all(partial_grad, ('freq', 'rep'), split_axis=2, concat_axis=1...]
    dot_general x20 -> x0, matrix products: 15.5 us -> none  [product(): return jnp.einsum(form, first, second, preferred_element_type=jnp.float32)]
    all_to_all x1 -> x0, starting transfers between devices: 8.04 us -> none  [shards(): lax.all_to_all(spectrum, 'freq', split_axis=1, concat_axis=2, tiled=True)]
    another operation x6 -> x0, local copies, waits for them, and re-layouts: 7.6 us -> none  [the longest x2 3.91 us: shards(): jnp.stack([out_re, out_im]).reshape(2, pair_count, row_tiles * tile_size)]
    all_to_all x1 -> x0, waiting for transfers between devices: 6.07 us -> none  [shards(): lax.all_to_all(spectrum, 'freq', split_axis=1, concat_axis=2, tiled=True)]
  transfers between devices with their start and end apart: 2 -> 0, of which waited for: 2 -> 0; matrix products, arithmetic and copies ran while one was open for 1% -> 0% of each run, Pallas kernels for 0% -> 0%
where the time goes in v1:
time: 73.6 us; the launch traced here: 73 us
  Pallas kernels  64.6 us (88%)
  local copies, waits for them, and re-layouts  7.83 us (11%)
    pallas_call x1, Pallas kernels, shards(): pl.pallas_call(functools.partial(chain_kernel, dims), out_shape=(jax.Shap...  60.9 us
    unnamed x15, local copies, waits for them, and re-layouts  7.83 us
    pallas_call x1, Pallas kernels, shards(): pl.pallas_call(traces_kernel, grid=(steps,), out_shape=(jax.ShapeDtypeStr...  3.63 us

profile of v1, /device:TPU:1, one launch (start us, length us, event | category | flops | bytes accessed | tf_op | source)
XLA Modules:
  0.0 73.0 jit_solution(6366102936897560254)
XLA Ops:
  0.6 0.8 %copy.8.ranks_ref = s32[3,4,2]{2,1,0:T(4,128)S(1)} copy(s32[3,4,2]{1,2,0:T(2,128)} %param.9) | data formatting | bytes 192 | tf_op args[3]
  1.4 0.0 copy-start
  1.4 1.6 %copy-done = bf16[1,32,32,1024]{3,2,1,0:T(8,128)(2,1)S(1)} copy-done((bf16[1,32,32,1024]{3,2,1,0:T(8,128)(2,1)S(1)}, bf16[1,32,32,1024]{3,2,1,0:T(8,128)(2,1)}, u32[]{:S(2)}) %copy-start) | copy-done | bytes 2097176
  3.0 0.0 copy-start.1
  3.0 1.3 %copy-done.1 = bf16[2,3,4,2,48,256]{5,4,3,2,1,0:T(8,128)(2,1)S(1)} copy-done((bf16[2,3,4,2,48,256]{5,4,3,2,1,0:T(8,128)(2,1)S(1)}, bf16[2,3,4,2,48,256]{5,4,3,2,1,0:T(8,128)(2,1)}, u32[]{:S(2)}) %copy-start.1) | copy-done | bytes 1179672
  4.3 0.0 copy-start.2
  4.3 1.3 %copy-done.2 = bf16[2,3,4,2,48,256]{5,4,3,2,1,0:T(8,128)(2,1)S(1)} copy-done((bf16[2,3,4,2,48,256]{5,4,3,2,1,0:T(8,128)(2,1)S(1)}, bf16[2,3,4,2,48,256]{5,4,3,2,1,0:T(8,128)(2,1)}, u32[]{:S(2)}) %copy-start.2) | copy-done | bytes 1179672
  5.5 0.0 copy-start.3
  5.5 0.9 %copy-done.3 = bf16[96,1024]{1,0:T(8,128)(2,1)S(1)} copy-done((bf16[96,1024]{1,0:T(8,128)(2,1)S(1)}, bf16[96,1024]{1,0:T(8,128)(2,1)}, u32[]{:S(2)}) %copy-start.3) | copy-done | bytes 196632
  6.5 0.0 copy-start.5
  6.5 0.8 %copy-done.5 = f32[2,4,1024]{2,1,0:T(4,128)S(1)} copy-done((f32[2,4,1024]{2,1,0:T(4,128)S(1)}, f32[2,4,1024]{2,1,0:T(4,128)}, u32[]{:S(2)}) %copy-start.5) | copy-done | bytes 32792
  7.2 60.9 %shard_map.77 = (f32[2,4,1024]{2,1,0:T(4,128)S(1)}, bf16[96,512]{1,0:T(8,128)(2,1)S(1)}) custom-call(bf16[1,32,32,1024]{3,2,1,0:T(8,128)(2,1)S(1)} %copy-done, bf16[2,3,4,2,48,256]{5,4,3,2,1,0:T(8,128)(2,1)S(1)} %copy-done.1, bf16[2,3,4,2,48,256]{5,4,3,2,1,0:T(8,128)(2,1)S(1)} %copy-done.2, s32[3,4,2]{2,1,0:T(4,128)S(1)} %copy.8.ranks_ref, ...), custom_call_target="tpu_custom_call" | custom-call | tf_op jit(solution)/shard_map/pallas_call | solution.py:413
  68.2 0.0 copy-start.4
  68.2 0.6 copy-done.4
  68.8 0.0 copy-start.6
  68.8 0.6 copy-done.6
  69.4 3.6 %shard_map.78 = (f32[2,4,1024]{2,1,0:T(4,128)}, bf16[1,16,32,1024]{3,2,1,0:T(8,128)(2,1)}) custom-call(bf16[96,512]{1,0:T(8,128)(2,1)} %copy-done.4, bf16[96,1024]{1,0:T(8,128)(2,1)} %constant.2.clone.table_ref, f32[2,4,1024]{2,1,0:T(4,128)} %copy-done.6), custom_call_target="tpu_custom_call" | custom-call | tf_op jit(solution)/shard_map/pallas_call | solution.py:463
Async XLA Ops:
  1.4 1.6 %copy-start = (bf16[1,32,32,1024]{3,2,1,0:T(8,128)(2,1)S(1)}, bf16[1,32,32,1024]{3,2,1,0:T(8,128)(2,1)}, u32[]{:S(2)}) copy-start(bf16[1,32,32,1024]{3,2,1,0:T(8,128)(2,1)} %model_ref.1) | copy-start | bytes 6291460
  3.0 1.3 %copy-start.1 = (bf16[2,3,4,2,48,256]{5,4,3,2,1,0:T(8,128)(2,1)S(1)}, bf16[2,3,4,2,48,256]{5,4,3,2,1,0:T(8,128)(2,1)}, u32[]{:S(2)}) copy-start(bf16[2,3,4,2,48,256]{5,4,3,2,1,0:T(8,128)(2,1)} %left_ref.1) | copy-start | bytes 3538948
  4.3 1.3 %copy-start.2 = (bf16[2,3,4,2,48,256]{5,4,3,2,1,0:T(8,128)(2,1)S(1)}, bf16[2,3,4,2,48,256]{5,4,3,2,1,0:T(8,128)(2,1)}, u32[]{:S(2)}) copy-start(bf16[2,3,4,2,48,256]{5,4,3,2,1,0:T(8,128)(2,1)} %right_ref.1) | copy-start | bytes 3538948
  5.5 0.9 %copy-start.3 = (bf16[96,1024]{1,0:T(8,128)(2,1)S(1)}, bf16[96,1024]{1,0:T(8,128)(2,1)}, u32[]{:S(2)}) copy-start(bf16[96,1024]{1,0:T(8,128)(2,1)} %constant.2.clone.table_ref) | copy-start | bytes 589828
  6.5 0.8 %copy-start.5 = (f32[2,4,1024]{2,1,0:T(4,128)S(1)}, f32[2,4,1024]{2,1,0:T(4,128)}, u32[]{:S(2)}) copy-start(f32[2,4,1024]{2,1,0:T(4,128)} %data_ref.1) | copy-start | bytes 98308
  68.2 0.6 copy-start.4
  68.8 0.6 copy-start.6

commit v2 on v1

--- a/solution.py
+++ b/solution.py
@@ -58,7 +58,9 @@
     send_r,
     recv_sib,
     send_z,
-    recv_z,
+    near_z,
+    far_z,
+    data,
     recv_d,
     back,
     grads,
@@ -67,11 +69,13 @@
     load_sem,
     out_sem,
     a_sem,
+    g_sem,
     sib_sem,
-    z_sem,
-    d_sem,
+    near_sem,
+    far_sem,
+    data_sem,
+    near_d_sem,
     swap_sem,
-    g_sem,
 ):
     n_freq, n_rtile, n_rep = dims
     n_z = n_rtile // 2
@@ -82,12 +86,25 @@
     me_slot = me_f * n_rep + me_p
     me_z = me_t // 2
     me_c = me_t % 2
+    me_k = me_z % 4
+    me_b = me_z // 4
     sibling = {"rtile": me_z * 2 + (1 - me_c)}
     group = model_ref.shape[1] // n_rep
     freq_local, row_tiles, col_tiles, rank_size, tile_size = right.shape[1:]
 
     def slot_device(slot):
         return {"freq": slot // n_rep, "rep": slot % n_rep}
+
+    def hops(shift):
+        return min(shift[0], 8 - shift[0]) + min(shift[1], 4 - shift[1])
+
+    shifts = sorted(((dy, dx) for dy in range(8) for dx in range(4)), key=hops)[:0:-1]
+    me_y = me_p * 4 + me_f // 4
+    me_x = me_f % 4
+    peers = []
+    for dy, dx in shifts:
+        y = (me_y + dy) % 8
+        peers.append((y % 4 * 4 + (me_x + dx) % 4) * 2 + y // 4)
 
     def z_device(z):
         return {"rtile": z * 2 + me_c}
@@ -103,8 +120,8 @@
             device_id_type=MESH,
         )
 
-    def zs_like(send_sem, recv_sem):
-        most = recv_z.at[pl.ds(0, n_z - 1)]
+    def chunks_like(count, send_sem, recv_sem):
+        most = recv_sib.at[pl.ds(0, count)]
         return pltpu.make_async_remote_copy(
             src_ref=most,
             dst_ref=most,
@@ -122,27 +139,23 @@
     left_load = pltpu.make_async_copy(left_ref, left, load_sem.at[3])
     model_load.start()
     table_load.start()
+    data_load = pltpu.make_async_copy(data_ref, data.at[me_b], load_sem.at[4])
+
+    barrier = pltpu.get_barrier_semaphore()
+
+    for slot in peers:
+        pl.semaphore_signal(barrier, inc=1, device_id=slot_device(slot), device_id_type=MESH)
+    for shift in (1, 2, 4, n_z - 4, n_z - 2, n_z - 1):
+        pl.semaphore_signal(
+            barrier, inc=1, device_id=z_device((me_z + shift) % n_z), device_id_type=MESH
+        )
+    pl.semaphore_signal(barrier, inc=1, device_id=sibling, device_id_type=MESH)
+
+    data_load.start()
+    table_load.wait()
+    model_load.wait()
     right_load.start()
     left_load.start()
-
-    barrier = pltpu.get_barrier_semaphore()
-
-    @pl.loop(1, n_slot)
-    def _(step):
-        pl.semaphore_signal(
-            barrier, inc=1, device_id=slot_device((me_slot + step) % n_slot), device_id_type=MESH
-        )
-
-    @pl.loop(1, n_z)
-    def _(step):
-        pl.semaphore_signal(
-            barrier, inc=1, device_id=z_device((me_z + step) % n_z), device_id_type=MESH
-        )
-
-    pl.semaphore_signal(barrier, inc=1, device_id=sibling, device_id_type=MESH)
-
-    table_load.wait()
-    model_load.wait()
     bins = n_freq * freq_local
     traces_2d = traces[...].reshape(group * traces.shape[1], traces.shape[2])
     spectra = matmul(LAST, table[...], traces_2d)
@@ -173,7 +186,7 @@
     band = freq_local * 8
     send_a[...] = stage[...].reshape(n_freq, band, 128).astype(BF16)
 
-    pl.semaphore_wait(barrier, n_slot - 1 + n_z)
+    pl.semaphore_wait(barrier, n_slot - 1 + 7)
 
     def a_copy(target, source):
         return pltpu.make_async_remote_copy(
@@ -185,9 +198,22 @@
             device_id_type=MESH,
         )
 
-    @pl.loop(1, n_slot)
-    def _(step):
-        a_copy((me_slot + step) % n_slot, me_slot).start()
+    for slot in peers:
+        a_copy(slot, me_slot).start()
+
+    def data_copy(shift, send_sem):
+        return pltpu.make_async_remote_copy(
+            src_ref=data.at[me_b],
+            dst_ref=data.at[me_b],
+            send_sem=send_sem,
+            recv_sem=data_sem,
+            device_id=z_device((me_z + shift) % n_z),
+            device_id_type=MESH,
+        )
+
+    data_load.wait()
+    data_copy(4, out_sem.at[6]).start()
+    data_copy(n_z - 4, out_sem.at[6]).start()
 
     recv_a[me_slot] = send_a[me_f]
     right_load.wait()
@@ -198,6 +224,19 @@
     per_tile = n_slot // col_tiles
     lane_p = lanes((row_tiles * rank_size, 128))
     row_k = rows((rank_size, 128))
+    low4 = rows((32, tile_size)) % 8 < 4
+
+    def sib_copy(f):
+        part = pl.ds(f * 4, 4)
+        return pltpu.make_async_remote_copy(
+            src_ref=send_r.at[1 - me_c, part],
+            dst_ref=recv_sib.at[part],
+            send_sem=out_sem.at[1],
+            recv_sem=sib_sem.at[f],
+            device_id=sibling,
+            device_id_type=MESH,
+        )
+
     for f in range(freq_local):
         for j in range(col_tiles):
             arrived = recv_a[j * per_tile : (j + 1) * per_tile, f * 8 : (f + 1) * 8, :]
@@ -217,10 +256,8 @@
             for i in range(row_tiles):
                 part = projected[i * rank_size : (i + 1) * rank_size]
                 back[f, i, j * rank_size : (j + 1) * rank_size, :] = jnp.where(
-                    row_k < ranks_ref[f, i, j], part, 0.0
+                    row_k < ranks_ref[f, j, i], part, 0.0
                 )
-    low4 = rows((32, tile_size)) % 8 < 4
-    for f in range(freq_local):
         for i in range(row_tiles):
             lhs = back[f, i].T[:64].astype(BF16)
             span = slice(i * tile_size, (i + 1) * tile_size)
@@ -232,76 +269,101 @@
             odd = jnp.where(low4, pltpu.roll(out_re, 28, 0), out_im)
             send_r[0, f * 4 : (f + 1) * 4, :, span] = even.reshape(4, 8, tile_size).astype(BF16)
             send_r[1, f * 4 : (f + 1) * 4, :, span] = odd.reshape(4, 8, tile_size).astype(BF16)
-
-    sib_copy = pltpu.make_async_remote_copy(
-        src_ref=send_r.at[1 - me_c],
-        dst_ref=recv_sib,
-        send_sem=out_sem.at[1],
-        recv_sem=sib_sem,
+        sib_copy(f).start()
+
+    half = send_r.shape[3] // 2
+    whole = pl.ds(0, 2 * half)
+    first_half = pl.ds(0, half)
+    second_half = pl.ds(half, half)
+    near = (
+        (1, 1, 0, whole),
+        (n_z - 1, 3, 1, whole),
+        (2, 2, 2, first_half),
+        (n_z - 2, 2, 2, second_half),
+    )
+    for f in range(freq_local):
+        part = pl.ds(f * 4, 4)
+        sib_copy(f).wait_recv()
+        send_z[part] = (send_r[me_c, part].astype(F32) + recv_sib[part].astype(F32)).astype(BF16)
+        for shift, ahead, place, span in near:
+            pltpu.make_async_remote_copy(
+                src_ref=send_z.at[f * 4 + (me_k + ahead) % 4, :, span],
+                dst_ref=near_z.at[place, f, :, span],
+                send_sem=out_sem.at[2],
+                recv_sem=near_sem.at[f],
+                device_id=z_device((me_z + shift) % n_z),
+                device_id_type=MESH,
+            ).start()
+
+    far_shifts = (4, n_z - 4)
+    for f in range(freq_local):
+        chunks_like(3, out_sem.at[2], near_sem.at[f]).wait_recv()
+        total = send_z[f * 4 + me_k].astype(F32)
+        for place in range(3):
+            total = total + near_z[place, f].astype(F32)
+        far_z[me_b, f] = total.astype(BF16)
+        for shift in far_shifts:
+            pltpu.make_async_remote_copy(
+                src_ref=far_z.at[me_b, f],
+                dst_ref=far_z.at[me_b, f],
+                send_sem=out_sem.at[3],
+                recv_sem=far_sem.at[f],
+                device_id=z_device((me_z + shift) % n_z),
+                device_id_type=MESH,
+            ).start()
+
+    most = data.at[pl.ds(0, 2)]
+    pltpu.make_async_remote_copy(
+        src_ref=most,
+        dst_ref=most,
+        send_sem=out_sem.at[6],
+        recv_sem=data_sem,
         device_id=sibling,
         device_id_type=MESH,
-    )
-    sib_copy.start()
-    sib_copy.wait_recv()
-    send_z[...] = (send_r[me_c].astype(F32) + recv_sib[...].astype(F32)).astype(BF16)
-
-    def z_copy(target, source):
-        return pltpu.make_async_remote_copy(
-            src_ref=send_z.at[target],
-            dst_ref=recv_z.at[source],
-            send_sem=out_sem.at[2],
-            recv_sem=z_sem,
-            device_id=z_device(target),
-            device_id_type=MESH,
-        )
-
-    @pl.loop(1, n_z)
-    def _(step):
-        z_copy((me_z + step) % n_z, me_z).start()
-
-    recv_z[me_z] = send_z[me_z]
-
-    zs_like(out_sem.at[2], z_sem).wait_recv()
-
-    total = recv_z[0].astype(F32)
-    for z in range(1, n_z):
-        total = total + recv_z[z].astype(F32)
-    residual_re = total[:4] - data_ref[0]
-    residual_im = total[4:] - data_ref[1]
-    residual_ref[0] = residual_re
-    residual_ref[1] = residual_im
-    recv_d[me_c, me_z] = jnp.concatenate([residual_re, residual_im], axis=0).astype(BF16)
-
-    def d_copy(target, source):
-        return pltpu.make_async_remote_copy(
-            src_ref=recv_d.at[me_c, source],
-            dst_ref=recv_d.at[me_c, source],
-            send_sem=out_sem.at[3],
-            recv_sem=d_sem,
-            device_id=z_device(target),
-            device_id_type=MESH,
-        )
-
-    @pl.loop(1, n_z)
-    def _(step):
-        d_copy((me_z + step) % n_z, me_z).start()
-
-    zs_like(out_sem.at[3], d_sem).wait_recv()
-
-    swap = pltpu.make_async_remote_copy(
-        src_ref=recv_d.at[me_c],
-        dst_ref=recv_d.at[me_c],
-        send_sem=out_sem.at[4],
-        recv_sem=swap_sem,
-        device_id=sibling,
-        device_id_type=MESH,
-    )
-    swap.start()
-    swap.wait_recv()
+    ).wait()
+    for f in range(freq_local):
+        chunks_like(2, out_sem.at[3], far_sem.at[f]).wait_recv()
+        total = far_z[0, f].astype(F32)
+        for b in range(1, freq_local):
+            total = total + far_z[b, f].astype(F32)
+        residual_re = total[:4] - data[f, 0]
+        residual_im = total[4:] - data[f, 1]
+        recv_d[me_c, f * 4 + me_k] = jnp.concatenate([residual_re, residual_im], axis=0).astype(
+            BF16
+        )
+        for shift, _, _, span in near:
+            pltpu.make_async_remote_copy(
+                src_ref=recv_d.at[me_c, f * 4 + me_k, :, span],
+                dst_ref=recv_d.at[me_c, f * 4 + me_k, :, span],
+                send_sem=out_sem.at[4],
+                recv_sem=near_d_sem.at[f],
+                device_id=z_device((me_z + shift) % n_z),
+                device_id_type=MESH,
+            ).start()
+        data[f, 0] = residual_re
+        data[f, 1] = residual_im
+    residual_store = pltpu.make_async_copy(data.at[me_b], residual_ref, load_sem.at[5])
+    residual_store.start()
+
+    def swap_copy(f):
+        part = pl.ds(f * 4, 4)
+        return pltpu.make_async_remote_copy(
+            src_ref=recv_d.at[me_c, part],
+            dst_ref=recv_d.at[me_c, part],
+            send_sem=out_sem.at[7],
+            recv_sem=swap_sem.at[f],
+            device_id=sibling,
+            device_id_type=MESH,
+        )
+
+    for f in range(freq_local):
+        chunks_like(3, out_sem.at[4], near_d_sem.at[f]).wait_recv()
+        swap_copy(f).start()
 
     low4 = rows((32, recv_d.shape[3])) % 8 < 4
     row_k = rows((rank_size, 128))
     for f in range(freq_local):
+        swap_copy(f).wait_recv()
         even = recv_d[0, f * 4 : (f + 1) * 4].astype(F32).reshape(32, -1)
         odd = recv_d[1, f * 4 : (f + 1) * 4].astype(F32).reshape(32, -1)
         mis_re = jnp.where(low4, even, pltpu.roll(odd, 4, 0))
@@ -317,7 +379,7 @@
             )
             for j in range(col_tiles):
                 grads[j, i * rank_size : (i + 1) * rank_size, :] = jnp.where(
-                    row_k < ranks_ref[f, i, j], part[j * rank_size : (j + 1) * rank_size], 0.0
+                    row_k < ranks_ref[f, j, i], part[j * rank_size : (j + 1) * rank_size], 0.0
                 )
         for j in range(col_tiles):
             lhs = grads[j].T.astype(BF16)
@@ -344,9 +406,8 @@
             device_id_type=MESH,
         )
 
-    @pl.loop(1, n_slot)
-    def _(step):
-        g_copy((me_slot + step) % n_slot, me_slot).start()
+    for slot in peers:
+        g_copy(slot, me_slot).start()
 
     recv_g[me_slot] = send_g[me_slot]
 
@@ -382,18 +443,34 @@
         spec_ref[bins:, chunk * 128 : (chunk + 1) * 128] = im.astype(BF16)
 
     slots_like(out_sem.at[0], a_sem).wait_send()
-    zs_like(out_sem.at[2], z_sem).wait_send()
-    zs_like(out_sem.at[3], d_sem).wait_send()
     slots_like(out_sem.at[5], g_sem).wait_send()
-    sib_copy.wait_send()
-    swap.wait_send()
-
-
-def traces_kernel(spec_ref, table_ref, raw_ref, residual_ref, gradient_ref):
-    residual_ref[...] = raw_ref[...]
+    for place, count in ((1, 12), (2, 9), (3, 6), (4, 9), (7, 12)):
+        chunks_like(count, out_sem.at[place], g_sem).wait_send()
+    residual_store.wait()
+
+
+def traces_kernel(spec_ref, raw_ref, table_ref, residual_ref, gradient_ref, table, out, sems):
+    table_load = pltpu.make_async_copy(table_ref, table, sems.at[0])
+    table_load.start()
+    residual_store = pltpu.make_async_copy(raw_ref, residual_ref, sems.at[1])
+    residual_store.start()
+    _, group, rhs_count, length = gradient_ref.shape
+    steps = out.shape[0]
+    part = group // steps
     lhs = spec_ref[...].astype(F32).T.astype(BF16)
-    out = matmul(PLAIN, lhs, table_ref[...])
-    gradient_ref[...] = out.reshape(gradient_ref.shape).astype(BF16)
+    table_load.wait()
+    stores = []
+    for step in range(steps):
+        some = lhs[step * part * rhs_count : (step + 1) * part * rhs_count]
+        out[step] = matmul(PLAIN, some, table[...]).reshape(part, rhs_count, length).astype(BF16)
+        store = pltpu.make_async_copy(
+            out.at[step], gradient_ref.at[0, pl.ds(step * part, part)], sems.at[2 + step]
+        )
+        store.start()
+        stores.append(store)
+    residual_store.wait()
+    for store in stores:
+        store.wait()
 
 
 def shards(dims, model, green_left, green_right, ranks, data):
@@ -407,6 +484,7 @@
     bins = n_freq * freq_local
     sources = row_tiles * tile_size
     assert (rhs_count, tile_size, group, col_tiles) == (32, 256, 16, 2)
+    assert dims == (16, 24, 2)
     assert n_z == freq_local * 4 and n_slot * group == col_tiles * tile_size
     table = jnp.asarray(tables(bins, length))
     band = freq_local * 8
@@ -417,15 +495,15 @@
             jax.ShapeDtypeStruct((2 * bins, group * rhs_count), BF16),
         ),
         in_specs=[
-            pl.BlockSpec(memory_space=pl.ANY),
-            pl.BlockSpec(memory_space=pl.ANY),
-            pl.BlockSpec(memory_space=pl.ANY),
+            pl.BlockSpec(memory_space=pltpu.HBM),
+            pl.BlockSpec(memory_space=pltpu.HBM),
+            pl.BlockSpec(memory_space=pltpu.HBM),
             pl.BlockSpec(memory_space=pltpu.SMEM),
-            pl.BlockSpec(memory_space=pltpu.VMEM),
-            pl.BlockSpec(memory_space=pl.ANY),
+            pl.BlockSpec(memory_space=pltpu.HBM),
+            pl.BlockSpec(memory_space=pltpu.HBM),
         ],
         out_specs=(
-            pl.BlockSpec(memory_space=pltpu.VMEM),
+            pl.BlockSpec(memory_space=pltpu.HBM),
             pl.BlockSpec(memory_space=pltpu.VMEM),
         ),
         scratch_shapes=[
@@ -440,43 +518,51 @@
             pltpu.VMEM((2, n_z, 8, sources), BF16),
             pltpu.VMEM((n_z, 8, sources), BF16),
             pltpu.VMEM((n_z, 8, sources), BF16),
-            pltpu.VMEM((n_z, 8, sources), BF16),
+            pltpu.VMEM((3, freq_local, 8, sources), BF16),
+            pltpu.VMEM((freq_local, freq_local, 8, sources), BF16),
+            pltpu.VMEM((freq_local, *data.shape), F32),
             pltpu.VMEM((2, n_z, 8, sources), BF16),
             pltpu.VMEM((freq_local, row_tiles, col_tiles * rank_size, 128), F32),
             pltpu.VMEM((col_tiles, row_tiles * rank_size, 128), F32),
             pltpu.VMEM((n_slot, band, 128), BF16),
             pltpu.VMEM((n_slot, band, 128), BF16),
-            pltpu.SemaphoreType.DMA((4,)),
             pltpu.SemaphoreType.DMA((6,)),
+            pltpu.SemaphoreType.DMA((8,)),
             pltpu.SemaphoreType.DMA,
             pltpu.SemaphoreType.DMA,
+            pltpu.SemaphoreType.DMA((freq_local,)),
+            pltpu.SemaphoreType.DMA((freq_local,)),
+            pltpu.SemaphoreType.DMA((freq_local,)),
             pltpu.SemaphoreType.DMA,
-            pltpu.SemaphoreType.DMA,
-            pltpu.SemaphoreType.DMA,
-            pltpu.SemaphoreType.DMA,
+            pltpu.SemaphoreType.DMA((freq_local,)),
+            pltpu.SemaphoreType.DMA((freq_local,)),
         ],
         compiler_params=pltpu.CompilerParams(
-            collective_id=0, has_side_effects=True, vmem_limit_bytes=48 * 1024 * 1024
+            collective_id=0, has_side_effects=True, vmem_limit_bytes=60 * 1024 * 1024
         ),
-    )(model, green_left, green_right, ranks, data, table)
+    )(model, green_left, green_right, jnp.swapaxes(ranks, 1, 2), data, table)
     steps = 4
     residual, gradient = pl.pallas_call(
         traces_kernel,
-        grid=(steps,),
         out_shape=(
             jax.ShapeDtypeStruct(data.shape, F32),
             jax.ShapeDtypeStruct((1, group, rhs_count, length), BF16),
         ),
         in_specs=[
-            pl.BlockSpec((2 * bins, group * rhs_count // steps), lambda step: (0, step)),
-            pl.BlockSpec((2 * bins, length), lambda step: (0, 0)),
-            pl.BlockSpec(data.shape, lambda step: (0, 0, 0)),
+            pl.BlockSpec(memory_space=pltpu.VMEM),
+            pl.BlockSpec(memory_space=pltpu.VMEM),
+            pl.BlockSpec(memory_space=pltpu.HBM),
         ],
         out_specs=(
-            pl.BlockSpec(data.shape, lambda step: (0, 0, 0)),
-            pl.BlockSpec((1, group // steps, rhs_count, length), lambda step: (0, step, 0, 0)),
+            pl.BlockSpec(memory_space=pltpu.HBM),
+            pl.BlockSpec(memory_space=pltpu.HBM),
         ),
-    )(spec, table, raw)
+        scratch_shapes=[
+            pltpu.VMEM((2 * bins, length), BF16),
+            pltpu.VMEM((steps, group // steps, rhs_count, length), BF16),
+            pltpu.SemaphoreType.DMA((2 + steps,)),
+        ],
+    )(spec, raw, table)
     return (residual, gradient)
 
 

time: 73.6 us -> 59.7 us (0.81)
  local copies, waits for them, and re-layouts: 7.83 us -> 0 us
  Pallas kernels: 64.6 us -> 58.8 us
    unnamed x15 -> x0, local copies, waits for them, and re-layouts: 7.83 us -> none
    pallas_call x1, Pallas kernels: 60.9 us -> 55.8 us  [shards(): pl.pallas_call(functools.partial(chain_kernel, dims), out_shape=(jax.Shap...]
where the time goes in v2:
time: 59.7 us; the launch traced here: 59.5 us
  Pallas kernels  58.8 us (98%)
  between operations  0.64 us (1%)
    pallas_call x1, Pallas kernels, shards(): pl.pallas_call(functools.partial(chain_kernel, dims), out_shape=(jax.Shap...  55.8 us
    pallas_call x1, Pallas kernels, shards(): pl.pallas_call(traces_kernel, out_shape=(jax.ShapeDtypeStruct(data.shape,...  3.06 us

profile of v2, /device:TPU:1, one launch (start us, length us, event | category | flops | bytes accessed | tf_op | source)
XLA Modules:
  0.0 59.5 jit_solution(14744728920968071766)
XLA Ops:
  0.6 55.8 %shard_map.77 = (f32[2,4,1024]{2,1,0:T(4,128)}, bf16[96,512]{1,0:T(8,128)(2,1)}) custom-call(bf16[1,32,32,1024]{3,2,1,0:T(8,128)(2,1)} %model_ref.1, bf16[2,3,4,2,48,256]{5,4,3,2,1,0:T(8,128)(2,1)} %left_ref.1, bf16[2,3,4,2,48,256]{5,4,3,2,1,0:T(8,128)(2,1)} %right_ref.1, s32[3,2,4]{2,1,0:T(2,128)} %bitcast.1, f32[2,4,1024]{2,1,0:T(4,128)} %data_ref.1, ...), custom_call_target="tpu_custom_call" | custom-call | tf_op jit(solution)/shard_map/pallas_call | solution.py:491
  56.4 3.1 %shard_map.78 = (f32[2,4,1024]{2,1,0:T(4,128)}, bf16[1,16,32,1024]{3,2,1,0:T(8,128)(2,1)}) custom-call(bf16[96,512]{1,0:T(8,128)(2,1)} %get-tuple-element.4.spec_ref, f32[2,4,1024]{2,1,0:T(4,128)} %get-tuple-element.5.raw_ref, bf16[96,1024]{1,0:T(8,128)(2,1)} %constant.2.clone.table_ref), custom_call_target="tpu_custom_call" | custom-call | tf_op jit(solution)/shard_map/pallas_call | solution.py:545

commit v3 on v2

--- a/solution.py
+++ b/solution.py
@@ -42,11 +42,12 @@
     model_ref,
     left_ref,
     right_ref,
-    ranks_ref,
+    ranks_hbm,
     data_ref,
     table_ref,
     residual_ref,
     spec_ref,
+    ranks_ref,
     traces,
     table,
     left,
@@ -131,14 +132,22 @@
             device_id_type=MESH,
         )
 
-    model_load = pltpu.make_async_copy(
-        model_ref.at[0, pl.ds(me_p * group, group)], traces, load_sem.at[0]
-    )
+    half_group = group // 2
+    model_loads = [
+        pltpu.make_async_copy(
+            model_ref.at[0, pl.ds(me_p * group + part * half_group, half_group)],
+            traces.at[pl.ds(part * half_group, half_group)],
+            load_sem.at[6 + part],
+        )
+        for part in range(2)
+    ]
+    ranks_load = pltpu.make_async_copy(ranks_hbm, ranks_ref, load_sem.at[0])
     table_load = pltpu.make_async_copy(table_ref, table, load_sem.at[1])
     right_load = pltpu.make_async_copy(right_ref, right, load_sem.at[2])
     left_load = pltpu.make_async_copy(left_ref, left, load_sem.at[3])
-    model_load.start()
     table_load.start()
+    model_loads[0].start()
+    model_loads[1].start()
     data_load = pltpu.make_async_copy(data_ref, data.at[me_b], load_sem.at[4])
 
     barrier = pltpu.get_barrier_semaphore()
@@ -152,17 +161,22 @@
     pl.semaphore_signal(barrier, inc=1, device_id=sibling, device_id_type=MESH)
 
     data_load.start()
-    table_load.wait()
-    model_load.wait()
     right_load.start()
     left_load.start()
+    ranks_load.start()
+
+    table_load.wait()
     bins = n_freq * freq_local
-    traces_2d = traces[...].reshape(group * traces.shape[1], traces.shape[2])
-    spectra = matmul(LAST, table[...], traces_2d)
     quarter = lanes((bins, 128)) // 32
     for chunk in range(group // 4):
-        re = spectra[:bins, chunk * 128 : (chunk + 1) * 128]
-        im = spectra[bins:, chunk * 128 : (chunk + 1) * 128]
+        if chunk % 2 == 0:
+            part = chunk // 2
+            model_loads[part].wait()
+            some = traces[part * half_group : (part + 1) * half_group]
+            spectra = matmul(LAST, table[...], some.reshape(-1, traces.shape[2]))
+        at = chunk % 2 * 128
+        re = spectra[:bins, at : at + 128]
+        im = spectra[bins:, at : at + 128]
         first = jnp.where(
             quarter == 0,
             re,
@@ -218,6 +232,7 @@
     recv_a[me_slot] = send_a[me_f]
     right_load.wait()
     left_load.wait()
+    ranks_load.wait()
 
     slots_like(out_sem.at[0], a_sem).wait_recv()
 
@@ -237,7 +252,7 @@
             device_id_type=MESH,
         )
 
-    for f in range(freq_local):
+    def predict(f):
         for j in range(col_tiles):
             arrived = recv_a[j * per_tile : (j + 1) * per_tile, f * 8 : (f + 1) * 8, :]
             arrived = arrived.astype(F32).reshape(per_tile * 8, 128)
@@ -281,7 +296,7 @@
         (2, 2, 2, first_half),
         (n_z - 2, 2, 2, second_half),
     )
-    for f in range(freq_local):
+    def near_sends(f):
         part = pl.ds(f * 4, 4)
         sib_copy(f).wait_recv()
         send_z[part] = (send_r[me_c, part].astype(F32) + recv_sib[part].astype(F32)).astype(BF16)
@@ -294,6 +309,12 @@
                 device_id=z_device((me_z + shift) % n_z),
                 device_id_type=MESH,
             ).start()
+
+    predict(0)
+    for f in range(1, freq_local):
+        predict(f)
+        near_sends(f - 1)
+    near_sends(freq_local - 1)
 
     far_shifts = (4, n_z - 4)
     for f in range(freq_local):
@@ -449,22 +470,30 @@
     residual_store.wait()
 
 
-def traces_kernel(spec_ref, raw_ref, table_ref, residual_ref, gradient_ref, table, out, sems):
-    table_load = pltpu.make_async_copy(table_ref, table, sems.at[0])
+def traces_kernel(
+    spec_ref, raw_ref, table_ref, residual_ref, gradient_ref, spec, table, raw, out, sems
+):
+    spec_load = pltpu.make_async_copy(spec_ref, spec, sems.at[0])
+    table_load = pltpu.make_async_copy(table_ref, table, sems.at[1])
+    raw_load = pltpu.make_async_copy(raw_ref, raw, sems.at[2])
+    residual_store = pltpu.make_async_copy(raw, residual_ref, sems.at[3])
+    spec_load.start()
     table_load.start()
-    residual_store = pltpu.make_async_copy(raw_ref, residual_ref, sems.at[1])
-    residual_store.start()
+    raw_load.start()
     _, group, rhs_count, length = gradient_ref.shape
     steps = out.shape[0]
     part = group // steps
-    lhs = spec_ref[...].astype(F32).T.astype(BF16)
+    spec_load.wait()
+    lhs = spec[...].astype(F32).T.astype(BF16)
     table_load.wait()
+    raw_load.wait()
+    residual_store.start()
     stores = []
     for step in range(steps):
         some = lhs[step * part * rhs_count : (step + 1) * part * rhs_count]
         out[step] = matmul(PLAIN, some, table[...]).reshape(part, rhs_count, length).astype(BF16)
         store = pltpu.make_async_copy(
-            out.at[step], gradient_ref.at[0, pl.ds(step * part, part)], sems.at[2 + step]
+            out.at[step], gradient_ref.at[0, pl.ds(step * part, part)], sems.at[4 + step]
         )
         store.start()
         stores.append(store)
@@ -498,7 +527,7 @@
             pl.BlockSpec(memory_space=pltpu.HBM),
             pl.BlockSpec(memory_space=pltpu.HBM),
             pl.BlockSpec(memory_space=pltpu.HBM),
-            pl.BlockSpec(memory_space=pltpu.SMEM),
+            pl.BlockSpec(memory_space=pltpu.HBM),
             pl.BlockSpec(memory_space=pltpu.HBM),
             pl.BlockSpec(memory_space=pltpu.HBM),
         ],
@@ -507,6 +536,7 @@
             pl.BlockSpec(memory_space=pltpu.VMEM),
         ),
         scratch_shapes=[
+            pltpu.SMEM((freq_local, col_tiles, row_tiles), jnp.int32),
             pltpu.VMEM((group, rhs_count, length), BF16),
             pltpu.VMEM((2 * bins, length), BF16),
             pltpu.VMEM(green_left.shape, BF16),
@@ -526,7 +556,7 @@
             pltpu.VMEM((col_tiles, row_tiles * rank_size, 128), F32),
             pltpu.VMEM((n_slot, band, 128), BF16),
             pltpu.VMEM((n_slot, band, 128), BF16),
-            pltpu.SemaphoreType.DMA((6,)),
+            pltpu.SemaphoreType.DMA((8,)),
             pltpu.SemaphoreType.DMA((8,)),
             pltpu.SemaphoreType.DMA,
             pltpu.SemaphoreType.DMA,
@@ -549,8 +579,8 @@
             jax.ShapeDtypeStruct((1, group, rhs_count, length), BF16),
         ),
         in_specs=[
-            pl.BlockSpec(memory_space=pltpu.VMEM),
-            pl.BlockSpec(memory_space=pltpu.VMEM),
+            pl.BlockSpec(memory_space=pltpu.HBM),
+            pl.BlockSpec(memory_space=pltpu.HBM),
             pl.BlockSpec(memory_space=pltpu.HBM),
         ],
         out_specs=(
@@ -558,10 +588,13 @@
             pl.BlockSpec(memory_space=pltpu.HBM),
         ),
         scratch_shapes=[
+            pltpu.VMEM((2 * bins, group * rhs_count), BF16),
             pltpu.VMEM((2 * bins, length), BF16),
+            pltpu.VMEM(data.shape, F32),
             pltpu.VMEM((steps, group // steps, rhs_count, length), BF16),
-            pltpu.SemaphoreType.DMA((2 + steps,)),
+            pltpu.SemaphoreType.DMA((4 + steps,)),
         ],
+        compiler_params=pltpu.CompilerParams(vmem_limit_bytes=60 * 1024 * 1024),
     )(spec, raw, table)
     return (residual, gradient)
 

time: 59.7 us -> 58.4 us (0.978)
  Pallas kernels: 58.8 us -> 57.6 us
    pallas_call x1, Pallas kernels: 3.06 us -> 2.25 us  [shards(): pl.pallas_call(traces_kernel, out_shape=(jax.ShapeDtypeStruct(data.shape,...]
where the time goes in v3:
time: 58.4 us; the launch traced here: 58.2 us
  Pallas kernels  57.6 us (99%)
  between operations  0.64 us (1%)
    pallas_call x1, Pallas kernels, shards(): pl.pallas_call(functools.partial(chain_kernel, dims), out_shape=(jax.Shap...  55.3 us
    pallas_call x1, Pallas kernels, shards(): pl.pallas_call(traces_kernel, out_shape=(jax.ShapeDtypeStruct(data.shape,...  2.25 us

profile of v3, /device:TPU:1, one launch (start us, length us, event | category | flops | bytes accessed | tf_op | source)
XLA Modules:
  0.0 58.2 jit_solution(3923437737300424791)
XLA Ops:
  0.6 55.3 %shard_map.77 = (f32[2,4,1024]{2,1,0:T(4,128)}, bf16[96,512]{1,0:T(8,128)(2,1)}) custom-call(bf16[1,32,32,1024]{3,2,1,0:T(8,128)(2,1)} %model_ref.1, bf16[2,3,4,2,48,256]{5,4,3,2,1,0:T(8,128)(2,1)} %left_ref.1, bf16[2,3,4,2,48,256]{5,4,3,2,1,0:T(8,128)(2,1)} %right_ref.1, s32[3,2,4]{2,1,0:T(2,128)} %bitcast.1, f32[2,4,1024]{2,1,0:T(4,128)} %data_ref.1, ...), custom_call_target="tpu_custom_call" | custom-call | tf_op jit(solution)/shard_map/pallas_call | solution.py:520
  56.0 2.2 %shard_map.78 = (f32[2,4,1024]{2,1,0:T(4,128)}, bf16[1,16,32,1024]{3,2,1,0:T(8,128)(2,1)}) custom-call(bf16[96,512]{1,0:T(8,128)(2,1)} %get-tuple-element.4.spec_ref, f32[2,4,1024]{2,1,0:T(4,128)} %get-tuple-element.5.raw_ref, bf16[96,1024]{1,0:T(8,128)(2,1)} %constant.2.clone.table_ref), custom_call_target="tpu_custom_call" | custom-call | tf_op jit(solution)/shard_map/pallas_call | solution.py:575

commit v4 on v3

--- a/solution.py
+++ b/solution.py
@@ -291,10 +291,10 @@
     first_half = pl.ds(0, half)
     second_half = pl.ds(half, half)
     near = (
+        (2, 2, 2, first_half),
+        (n_z - 2, 2, 2, second_half),
         (1, 1, 0, whole),
         (n_z - 1, 3, 1, whole),
-        (2, 2, 2, first_half),
-        (n_z - 2, 2, 2, second_half),
     )
     def near_sends(f):
         part = pl.ds(f * 4, 4)

time: 58.4 us -> 57.4 us (0.983)
  Pallas kernels: 57.6 us -> 56.6 us
    pallas_call x1, Pallas kernels: 55.3 us -> 54.3 us  [shards(): pl.pallas_call(functools.partial(chain_kernel, dims), out_shape=(jax.Shap...]
where the time goes in v4:
time: 57.4 us; the launch traced here: 57.2 us
  Pallas kernels  56.6 us (99%)
  between operations  0.64 us (1%)
    pallas_call x1, Pallas kernels, shards(): pl.pallas_call(functools.partial(chain_kernel, dims), out_shape=(jax.Shap...  54.3 us
    pallas_call x1, Pallas kernels, shards(): pl.pallas_call(traces_kernel, out_shape=(jax.ShapeDtypeStruct(data.shape,...  2.25 us

profile of v4, /device:TPU:1, one launch (start us, length us, event | category | flops | bytes accessed | tf_op | source)
XLA Modules:
  0.0 57.2 jit_solution(9861509086499215402)
XLA Ops:
  0.6 54.3 %shard_map.77 = (f32[2,4,1024]{2,1,0:T(4,128)}, bf16[96,512]{1,0:T(8,128)(2,1)}) custom-call(bf16[1,32,32,1024]{3,2,1,0:T(8,128)(2,1)} %model_ref.1, bf16[2,3,4,2,48,256]{5,4,3,2,1,0:T(8,128)(2,1)} %left_ref.1, bf16[2,3,4,2,48,256]{5,4,3,2,1,0:T(8,128)(2,1)} %right_ref.1, s32[3,2,4]{2,1,0:T(2,128)} %bitcast.1, f32[2,4,1024]{2,1,0:T(4,128)} %data_ref.1, ...), custom_call_target="tpu_custom_call" | custom-call | tf_op jit(solution)/shard_map/pallas_call | solution.py:520
  55.0 2.2 %shard_map.78 = (f32[2,4,1024]{2,1,0:T(4,128)}, bf16[1,16,32,1024]{3,2,1,0:T(8,128)(2,1)}) custom-call(bf16[96,512]{1,0:T(8,128)(2,1)} %get-tuple-element.4.spec_ref, f32[2,4,1024]{2,1,0:T(4,128)} %get-tuple-element.5.raw_ref, bf16[96,1024]{1,0:T(8,128)(2,1)} %constant.2.clone.table_ref), custom_call_target="tpu_custom_call" | custom-call | tf_op jit(solution)/shard_map/pallas_call | solution.py:575

commit v5 on v4

--- a/solution.py
+++ b/solution.py
@@ -85,30 +85,33 @@
     me_t = lax.axis_index("rtile")
     me_p = lax.axis_index("rep")
     me_slot = me_f * n_rep + me_p
-    me_z = me_t // 2
-    me_c = me_t % 2
-    me_k = me_z % 4
-    me_b = me_z // 4
+    me_z = lax.div(me_t, 2)
+    me_c = lax.rem(me_t, 2)
+    me_k = lax.rem(me_z, 4)
+    me_b = lax.div(me_z, 4)
     sibling = {"rtile": me_z * 2 + (1 - me_c)}
     group = model_ref.shape[1] // n_rep
     freq_local, row_tiles, col_tiles, rank_size, tile_size = right.shape[1:]
 
     def slot_device(slot):
-        return {"freq": slot // n_rep, "rep": slot % n_rep}
+        return {"freq": lax.div(slot, n_rep), "rep": lax.rem(slot, n_rep)}
 
     def hops(shift):
         return min(shift[0], 8 - shift[0]) + min(shift[1], 4 - shift[1])
 
     shifts = sorted(((dy, dx) for dy in range(8) for dx in range(4)), key=hops)[:0:-1]
-    me_y = me_p * 4 + me_f // 4
-    me_x = me_f % 4
+    me_y = me_p * 4 + lax.div(me_f, 4)
+    me_x = lax.rem(me_f, 4)
     peers = []
     for dy, dx in shifts:
-        y = (me_y + dy) % 8
-        peers.append((y % 4 * 4 + (me_x + dx) % 4) * 2 + y // 4)
+        y = lax.rem(me_y + dy, 8)
+        peers.append((lax.rem(y, 4) * 4 + lax.rem(me_x + dx, 4)) * 2 + lax.div(y, 4))
 
     def z_device(z):
         return {"rtile": z * 2 + me_c}
+
+    def z_other(z):
+        return {"rtile": z * 2 + (1 - me_c)}
 
     def slots_like(send_sem, recv_sem):
         most = recv_a.at[pl.ds(0, n_slot - 1)]
@@ -154,9 +157,13 @@
 
     for slot in peers:
         pl.semaphore_signal(barrier, inc=1, device_id=slot_device(slot), device_id_type=MESH)
+    for shift in (1, 2, n_z - 2, n_z - 1):
+        pl.semaphore_signal(
+            barrier, inc=1, device_id=z_other(lax.rem(me_z + shift, n_z)), device_id_type=MESH
+        )
     for shift in (1, 2, 4, n_z - 4, n_z - 2, n_z - 1):
         pl.semaphore_signal(
-            barrier, inc=1, device_id=z_device((me_z + shift) % n_z), device_id_type=MESH
+            barrier, inc=1, device_id=z_device(lax.rem(me_z + shift, n_z)), device_id_type=MESH
         )
     pl.semaphore_signal(barrier, inc=1, device_id=sibling, device_id_type=MESH)
 
@@ -200,11 +207,11 @@
     band = freq_local * 8
     send_a[...] = stage[...].reshape(n_freq, band, 128).astype(BF16)
 
-    pl.semaphore_wait(barrier, n_slot - 1 + 7)
+    pl.semaphore_wait(barrier, n_slot - 1 + 11)
 
     def a_copy(target, source):
         return pltpu.make_async_remote_copy(
-            src_ref=send_a.at[target // n_rep],
+            src_ref=send_a.at[lax.div(target, n_rep)],
             dst_ref=recv_a.at[source],
             send_sem=out_sem.at[0],
             recv_sem=a_sem,
@@ -221,7 +228,7 @@
             dst_ref=data.at[me_b],
             send_sem=send_sem,
             recv_sem=data_sem,
-            device_id=z_device((me_z + shift) % n_z),
+            device_id=z_device(lax.rem(me_z + shift, n_z)),
             device_id_type=MESH,
         )
 
@@ -302,11 +309,11 @@
         send_z[part] = (send_r[me_c, part].astype(F32) + recv_sib[part].astype(F32)).astype(BF16)
         for shift, ahead, place, span in near:
             pltpu.make_async_remote_copy(
-                src_ref=send_z.at[f * 4 + (me_k + ahead) % 4, :, span],
+                src_ref=send_z.at[f * 4 + lax.rem(me_k + ahead, 4), :, span],
                 dst_ref=near_z.at[place, f, :, span],
                 send_sem=out_sem.at[2],
                 recv_sem=near_sem.at[f],
-                device_id=z_device((me_z + shift) % n_z),
+                device_id=z_device(lax.rem(me_z + shift, n_z)),
                 device_id_type=MESH,
             ).start()
 
@@ -329,7 +336,7 @@
                 dst_ref=far_z.at[me_b, f],
                 send_sem=out_sem.at[3],
                 recv_sem=far_sem.at[f],
-                device_id=z_device((me_z + shift) % n_z),
+                device_id=z_device(lax.rem(me_z + shift, n_z)),
                 device_id_type=MESH,
             ).start()
 
@@ -358,7 +365,25 @@
                 dst_ref=recv_d.at[me_c, f * 4 + me_k, :, span],
                 send_sem=out_sem.at[4],
                 recv_sem=near_d_sem.at[f],
-                device_id=z_device((me_z + shift) % n_z),
+                device_id=z_device(lax.rem(me_z + shift, n_z)),
+                device_id_type=MESH,
+            ).start()
+        if f == freq_local - 1:
+            for shift, _, _, span in near:
+                pltpu.make_async_remote_copy(
+                    src_ref=recv_d.at[me_c, f * 4 + me_k, :, span],
+                    dst_ref=recv_d.at[me_c, f * 4 + me_k, :, span],
+                    send_sem=out_sem.at[7],
+                    recv_sem=swap_sem.at[f],
+                    device_id=z_other(lax.rem(me_z + shift, n_z)),
+                    device_id_type=MESH,
+                ).start()
+            pltpu.make_async_remote_copy(
+                src_ref=recv_d.at[me_c, f * 4 + me_k],
+                dst_ref=recv_d.at[me_c, f * 4 + me_k],
+                send_sem=out_sem.at[7],
+                recv_sem=swap_sem.at[f],
+                device_id=sibling,
                 device_id_type=MESH,
             ).start()
         data[f, 0] = residual_re
@@ -379,7 +404,8 @@
 
     for f in range(freq_local):
         chunks_like(3, out_sem.at[4], near_d_sem.at[f]).wait_recv()
-        swap_copy(f).start()
+        if f < freq_local - 1:
+            swap_copy(f).start()
 
     low4 = rows((32, recv_d.shape[3])) % 8 < 4
     row_k = rows((rank_size, 128))

time: 57.4 us -> 57.2 us (level)
  no operation moved by 1% of the time
where the time goes in v5:
time: 57.2 us; the launch traced here: 57.1 us
  Pallas kernels  56.4 us (99%)
  between operations  0.64 us (1%)
    pallas_call x1, Pallas kernels, shards(): pl.pallas_call(functools.partial(chain_kernel, dims), out_shape=(jax.Shap...  54.2 us
    pallas_call x1, Pallas kernels, shards(): pl.pallas_call(traces_kernel, out_shape=(jax.ShapeDtypeStruct(data.shape,...  2.25 us

profile of v5, /device:TPU:1, one launch (start us, length us, event | category | flops | bytes accessed | tf_op | source)
XLA Modules:
  0.0 57.1 jit_solution(13267854162507061566)
XLA Ops:
  0.6 54.2 %shard_map.77 = (f32[2,4,1024]{2,1,0:T(4,128)}, bf16[96,512]{1,0:T(8,128)(2,1)}) custom-call(bf16[1,32,32,1024]{3,2,1,0:T(8,128)(2,1)} %model_ref.1, bf16[2,3,4,2,48,256]{5,4,3,2,1,0:T(8,128)(2,1)} %left_ref.1, bf16[2,3,4,2,48,256]{5,4,3,2,1,0:T(8,128)(2,1)} %right_ref.1, s32[3,2,4]{2,1,0:T(2,128)} %bitcast.1, f32[2,4,1024]{2,1,0:T(4,128)} %data_ref.1, ...), custom_call_target="tpu_custom_call" | custom-call | tf_op jit(solution)/shard_map/pallas_call | solution.py:546
  54.8 2.2 %shard_map.78 = (f32[2,4,1024]{2,1,0:T(4,128)}, bf16[1,16,32,1024]{3,2,1,0:T(8,128)(2,1)}) custom-call(bf16[96,512]{1,0:T(8,128)(2,1)} %get-tuple-element.4.spec_ref, f32[2,4,1024]{2,1,0:T(4,128)} %get-tuple-element.5.raw_ref, bf16[96,1024]{1,0:T(8,128)(2,1)} %constant.2.clone.table_ref), custom_call_target="tpu_custom_call" | custom-call | tf_op jit(solution)/shard_map/pallas_call | solution.py:601
